TPU v7x, 32 devices: a whole 2x2x4 slice. The times are simulated.
32 devices in a mesh: row: 2 (over x), col: 8 (over z, y), layer: 2 (over core).
Axes of the slice: x: 2, y: 2, z: 4, core: 2. Of those that a mesh axis runs over, the one named last changes fastest.
Arguments:
- owned_blocks: bfloat16 [512, 32, 128, 128], P(('row', 'col', 'layer')), may hold values from -1 to 1
- slot_rows: int32 [512], P(('row', 'col', 'layer')), may hold values from -1 to 255, as said below
- block_cols: int32 [512, 32], P(('row', 'col', 'layer')), may hold values from 0 to 255, as said below
Outputs:
- product_blocks: bfloat16 [256, 32, 128, 128], P(('row', 'layer'), 'col')
Inputs may be any that keep to these rules, and one draw needn't show every extreme that they name: `slot_rows`: every block row appears in exactly one slot. The 16 slots of the device at grid row r, grid column c and layer l (slots ((r * 8 + c) * 2 + l) * 16 onward) hold only block rows i with i // 128 = r and (i // 16) % 2 = l, or -1. In every grid row and layer some device uses all of its slots. block_cols[s, p] lies in panel p, between p * 8 and p * 8 + 7, also for unused slots.
All inputs are finite; a program needn't handle non-finite values.
Results may differ from a plain program's by a relative error of at most 0.001.
Values may be sent and summed in bfloat16 or wider, within the bound.
A program may use at most 256 MiB of HBM per device.

v0:
```python
import jax
import jax.numpy as jnp
from jax import lax
from jax.sharding import PartitionSpec as P

NB = 256


def grid_positions(row_ids, panels, panel_width, grid_row, rows_grid, layers, per_device):
    panel_index = row_ids // panel_width
    offset = row_ids % panel_width
    local_panel = panel_index - grid_row * (panels // rows_grid)
    layer_of = panel_index // per_device % layers
    half_rows = panels // rows_grid * panel_width // layers
    within = (
        local_panel // (per_device * layers) * per_device + local_panel % per_device
    ) * panel_width + offset
    placed = layer_of * half_rows + within
    return jnp.where(row_ids >= 0, placed, layers * half_rows).astype(jnp.int32)


def shards(owned_blocks, slot_rows, block_cols):
    own_slots = owned_blocks.shape[0]
    panels = owned_blocks.shape[1]
    block_size = owned_blocks.shape[2]
    rows_grid = lax.axis_size("row")
    cols_grid = lax.axis_size("col")
    layers = lax.axis_size("layer")
    per_device = panels // (cols_grid * layers)
    panel_width = NB // panels
    tile_rows = NB // rows_grid
    slots_here = layers * per_device
    outgoing = (
        owned_blocks.reshape(own_slots, cols_grid * layers, per_device, block_size, block_size),
        block_cols.reshape(own_slots, cols_grid * layers, per_device),
        jnp.broadcast_to(slot_rows[:, None], (own_slots, cols_grid * layers)),
        jnp.broadcast_to(block_cols[:, None, :], (own_slots, cols_grid * layers, panels)),
    )
    got_blocks, got_cols, got_rows, got_every = (
        lax.all_to_all(outgoing[0], ("col", "layer"), split_axis=1, concat_axis=0, tiled=True),
        lax.all_to_all(outgoing[1], ("col", "layer"), split_axis=1, concat_axis=0, tiled=True),
        lax.all_to_all(outgoing[2], ("col", "layer"), split_axis=1, concat_axis=0, tiled=True),
        lax.all_to_all(outgoing[3], ("col", "layer"), split_axis=1, concat_axis=0, tiled=True),
    )
    got_rows = got_rows.reshape(-1)
    slot_total = got_rows.shape[0]
    got_blocks = got_blocks.reshape(slot_total, per_device, block_size, block_size)
    got_cols = got_cols.reshape(slot_total, per_device)
    got_every = got_every.reshape(slot_total, panels)
    target = grid_positions(
        got_rows, panels, panel_width, lax.axis_index("row"), rows_grid, layers, per_device
    )
    row_tile = (
        jnp.zeros((tile_rows, per_device, block_size, block_size), jnp.bfloat16)
        .at[target]
        .set(got_blocks, mode="drop")
    )
    col_tile = jnp.zeros((tile_rows, per_device), jnp.int32).at[target].set(got_cols, mode="drop")
    every_cols = jnp.zeros((tile_rows, panels), jnp.int32).at[target].set(got_every, mode="drop")
    target_cols = lax.dynamic_slice_in_dim(
        every_cols, lax.axis_index("col") * slots_here, slots_here, 1
    )
    column_tile, column_ids = (
        lax.all_to_all(row_tile, "layer", split_axis=0, concat_axis=1, tiled=True),
        lax.all_to_all(col_tile, "layer", split_axis=0, concat_axis=1, tiled=True),
    )
    column_table, column_ids = (
        lax.all_gather(column_tile, "row", axis=0, tiled=True),
        lax.all_gather(column_ids, "row", axis=0, tiled=True),
    )
    column_table = column_table.reshape(
        panels // layers, panel_width, slots_here, block_size, block_size
    )
    column_ids = column_ids.reshape(panels // layers, panel_width, slots_here)
    initial = jnp.zeros((tile_rows, slots_here, block_size, block_size), jnp.float32)
    piece_blocks = lax.all_gather(row_tile, "col", axis=1, tiled=True)
    piece_cols = lax.all_gather(col_tile, "col", axis=1, tiled=True)
    panel_count = piece_blocks.shape[1]
    panel_steps = jnp.arange(panel_count, dtype=jnp.int32)
    offsets = piece_cols % panel_width

    def one_block(block_index):
        left_blocks = lax.dynamic_slice_in_dim(piece_blocks, block_index * 8, 8, 0)
        row_offsets = lax.dynamic_slice_in_dim(offsets, block_index * 8, 8, 0)
        wanted = lax.dynamic_slice_in_dim(target_cols, block_index * 8, 8, 0)
        chosen = column_table[panel_steps[None, :], row_offsets]
        chosen_ids = column_ids[panel_steps[None, :], row_offsets]
        matched = chosen_ids == wanted[:, None, :]
        chosen = jnp.where(matched[:, :, :, None, None], chosen, jnp.zeros((), jnp.bfloat16))
        return jnp.einsum(
            "mtab,mtsbc->msac", left_blocks, chosen, preferred_element_type=jnp.float32
        )

    products = lax.map(one_block, jnp.arange(tile_rows // 8, dtype=jnp.int32))
    partial_value = initial + products.reshape(initial.shape)
    own_rows = lax.psum_scatter(partial_value, "layer", scatter_dimension=0, tiled=True)
    return own_rows.astype(jnp.bfloat16)


def solution(mesh):
    return jax.shard_map(
        shards,
        mesh=mesh,
        in_specs=(
            P(("row", "col", "layer"), None, None, None),
            P(("row", "col", "layer")),
            P(("row", "col", "layer"), None),
        ),
        out_specs=P(("row", "layer"), "col", None, None),
        check_vma=False,
    )
```

profile of v0, /device:TPU:0, one launch (start us, length us, event | category | flops | bytes accessed | tf_op | source)
XLA Modules:
  0.0 2838.5 jit_solution(2040272807180117148)
XLA Ops:
  35.6 296.6 %all-to-all-done.4 = bf16[16,16,2,128,128]{4,3,2,0,1:T(8,128)(2,1)} async-done(((bf16[16,16,2,128,128]{4,3,2,0,1:T(8,128)(2,1)}), bf16[16,16,2,128,128]{4,3,2,0,1:T(8,128)(2,1)}, u32[]{:S(2)}, u32[]{:S(2)}) %all-to-all-start.4) | async-done | bytes 16777248 | tf_op jit(solution)/shard_map/all_to_all | solution.py:40
  337.7 42.9 %scatter_fusion = bf16[128,2,128,128]{3,2,1,0:T(8,128)(2,1)} fusion(bf16[128,2,128,128]{3,2,1,0:T(8,128)(2,1)} %broadcast_in_dim.81, s32[256]{0:T(256)S(1)} %bitcast.92, bf16[256,2,128,128]{3,2,1,0:T(8,128)(2,1)} %bitcast.21), kind=kCustom, calls=%fused_computation.4 | custom fusion | bytes 50332672 | tf_op jit(solution)/shard_map/scatter | solution.py:56
  380.6 18.7 all_to_all.95
  411.2 69.9 %all-to-all-start.1 = ((s32[16,16,2]{0,2,1:T(2,128)}), s32[16,16,2]{0,2,1:T(2,128)S(1)}, u32[]{:S(2)}, u32[]{:S(2)}) async-start(s32[16,16,2]{0,2,1:T(2,128)} %bitcast.2), calls=%async_computation.1 | async-start | bytes 32768 | tf_op jit(solution)/shard_map/all_to_all | solution.py:41
  522.3 151.9 %all-gather.5.cloned.1.call-done = bf16[128,4,128,128]{3,2,1,0:T(8,128)(2,1)} async-done(((bf16[64,4,128,128]{3,2,1,0:T(8,128)(2,1)}), bf16[128,4,128,128]{3,2,1,0:T(8,128)(2,1)}) %all-gather.5.cloned.1.call-update) | async-done | bytes 16777232 | tf_op jit(solution)/shard_map/all_gather | solution.py:68
  674.2 1268.5 %all-gather.7.cloned.1.call-done = bf16[128,16,128,128]{3,2,1,0:T(8,128)(2,1)} async-done(((bf16[128,2,128,128]{3,2,1,0:T(8,128)(2,1)}), bf16[128,16,128,128]{3,2,1,0:T(8,128)(2,1)}) %all-gather.7.cloned.1.call-update) | async-done | bytes 67108880 | tf_op jit(solution)/shard_map/all_gather | solution.py:76
  1942.7 835.0 %while.12 = (s32[]{:T(128)}, f32[16,8,4,128,128]{4,3,2,1,0:T(8,128)}, s32[16]{0:T(128)S(1)}, s32[128,16]{1,0:T(8,128)S(1)}, s32[16,8,4]{2,1,0:T(8,128)S(1)}, /*i...) while((s32[]{:T(128)}, ...), condition=%wide.region_4.5_spmd.clone, body=%wide.region_3.4_spmd.clone.sunk | while | flops 2155873536 | bytes 98579704 | solution.py:94
  1959.6 21.6 copy.57
  2011.7 21.6 copy.57
  2064.0 21.6 copy.57
  2116.2 21.6 copy.57
  2168.3 21.6 copy.57
  2220.5 21.6 copy.57
  2272.8 21.6 copy.57
  2325.0 21.6 copy.57
  2377.2 21.6 copy.57
  2429.3 21.6 copy.57
  2481.6 21.6 copy.57
  2533.7 21.6 copy.57
  2585.9 21.6 copy.57
  2638.0 21.6 copy.57
  2690.2 21.6 copy.57
  2742.4 21.6 copy.57
  2777.7 45.1 %reduce-scatter.2.cloned.1.call-done = f32[64,4,128,128]{3,2,1,0:T(8,128)} async-done(((f32[128,4,128,128]{3,2,1,0:T(8,128)}), f32[64,4,128,128]{3,2,1,0:T(8,128)}) %reduce-scatter.2.cloned.1.call-update) | async-done | bytes 16777232 | tf_op jit(solution)/shard_map/reduce_scatter | solution.py:96
  (238 shorter events, 575.4 us)
Async XLA Ops:
  7.8 21.5 all-to-all-start
  29.3 302.8 %all-to-all-start.4 = ((bf16[16,16,2,128,128]{4,3,2,0,1:T(8,128)(2,1)}), bf16[16,16,2,128,128]{4,3,2,0,1:T(8,128)(2,1)}, u32[]{:S(2)}, u32[]{:S(2)}) async-start(bf16[16,16,2,128,128]{4,3,2,0,1:T(8,128)(2,1)} %copy.39), calls=%async_computation.4 | async-start | bytes 33554432 | tf_op jit(solution)/shard_map/all_to_all | solution.py:40
  35.4 638.8 %all-gather.5.cloned.1.call-start = ((), (), s32[]{:S(2)}) async-start(), calls=%async_computation.7 | async-start | bytes 25165824 | tf_op jit(solution)/shard_map/all_gather | solution.py:68
  399.3 11.2 copy-start
  409.8 1532.9 %all-gather.7.cloned.1.call-start = ((), (), s32[]{:S(2)}) async-start(), calls=%async_computation.8 | async-start | bytes 75497472 | tf_op jit(solution)/shard_map/all_gather | solution.py:76
  411.2 76.4 %all-to-all-start.1 = ((s32[16,16,2]{0,2,1:T(2,128)}), s32[16,16,2]{0,2,1:T(2,128)S(1)}, u32[]{:S(2)}, u32[]{:S(2)}) async-start(s32[16,16,2]{0,2,1:T(2,128)} %bitcast.2), calls=%async_computation.1 | async-start | bytes 32768 | tf_op jit(solution)/shard_map/all_to_all | solution.py:41
  489.8 20.1 all-to-all-start.2
  509.9 10.1 all-to-all-start.3
  513.4 2309.4 %reduce-scatter.2.cloned.1.call-start = ((), (), s32[]{:S(2)}) async-start(), calls=%async_computation.9 | async-start | bytes 50331648 | tf_op jit(solution)/shard_map/reduce_scatter | solution.py:96
Sparse Core Ops, SparseCore 0:
  409.9 264.2 all-gather.4
  675.7 1266.9 all-gather.6
  2777.8 44.9 reduce-scatter.1
where the time goes:
time: 2850 us; the launch traced here: 2840 us
  waiting for transfers between devices  1770 us (62%)
  local copies, waits for them, and re-layouts  738 us (26%)
  matrix products  165 us (6%)
  starting transfers between devices  90.2 us (3%)
  blocking collectives  39.9 us (1%)
    all_gather x1, waiting for transfers between devices, shards(): piece_blocks = lax.all_gather(row_tile, 'col', axis=1, tiled=True)  1270 us
    gather x32, local copies, waits for them, and re-layouts, one_block(): chosen = column_table[panel_steps[None, :], row_offsets]  575 us
    all_to_all x1, waiting for transfers between devices, shards(): lax.all_to_all(outgoing[0], ('col', 'layer'), split_axis=1, concat_axis=0...  297 us
    dot_general x16, matrix products, one_block(): jnp.einsum('mtab,mtsbc->msac', left_blocks, chosen, preferred_element_typ...  165 us
    all_gather x1, waiting for transfers between devices, shards(): lax.all_gather(column_tile, 'row', axis=0, tiled=True)  152 us
    all_to_all x1, starting transfers between devices, shards(): lax.all_to_all(outgoing[1], ('col', 'layer'), split_axis=1, concat_axis=0...  69.9 us
  transfers between devices with their start and end apart: 8, of which 6 were waited for; matrix products, arithmetic and copies ran while one was open for 1% of the time, Pallas kernels for 0%

commit v1 on v0

--- a/solution.py
+++ b/solution.py
@@ -4,6 +4,28 @@
 from jax.sharding import PartitionSpec as P
 
 NB = 256
+
+
+def joined_along(blocks, dim):
+    blocks = jnp.moveaxis(blocks, 0, dim)
+    dims = blocks.shape
+    return blocks.reshape(*dims[:dim], dims[dim] * dims[dim + 1], *dims[dim + 2 :])
+
+
+def collected_by_bits(x, axis):
+    size = lax.axis_size(axis)
+    tiles = x[None]
+    for level in range(size.bit_length() - 1):
+        bit = 1 << level
+        other = lax.ppermute(tiles, axis, [(i, i ^ bit) for i in range(size)])
+        both = jnp.stack([tiles, other])
+        upper = lax.axis_index(axis) >> level & 1
+        tiles = jnp.where(upper == 0, both, both[::-1]).reshape(-1, *x.shape)
+    return tiles
+
+
+def gather_by_bits(x, axis, dim):
+    return joined_along(collected_by_bits(x, axis), dim)
 
 
 def grid_positions(row_ids, panels, panel_width, grid_row, rows_grid, layers, per_device):
@@ -65,7 +87,7 @@
         lax.all_to_all(col_tile, "layer", split_axis=0, concat_axis=1, tiled=True),
     )
     column_table, column_ids = (
-        lax.all_gather(column_tile, "row", axis=0, tiled=True),
+        gather_by_bits(column_tile, "row", 0),
         lax.all_gather(column_ids, "row", axis=0, tiled=True),
     )
     column_table = column_table.reshape(

time: 2850 us -> 2620 us (0.919)
  waiting for transfers between devices: 1770 us -> 1450 us
  starting transfers between devices: 90.2 us -> 149 us
    all_gather x1, waiting for transfers between devices: 1270 us -> 1100 us  [shards(): piece_blocks = lax.all_gather(row_tile, 'col', axis=1, tiled=True)]
    all_gather x1 -> x0, waiting for transfers between devices: 152 us -> none  [shards(): lax.all_gather(column_tile, 'row', axis=0, tiled=True)]
    all_to_all x1, starting transfers between devices: 3.22 us -> 59.9 us  [shards(): lax.all_to_all(col_tile, 'layer', split_axis=0, concat_axis=1, tiled=True)]
  transfers between devices with their start and end apart: 8 -> 8, of which waited for: 6 -> 5; matrix products, arithmetic and copies ran while one was open for 1% -> 2% of each run, Pallas kernels for 0% -> 0%
where the time goes in v1:
time: 2620 us; the launch traced here: 2610 us
  waiting for transfers between devices  1450 us (55%)
  local copies, waits for them, and re-layouts  738 us (28%)
  matrix products  165 us (6%)
  starting transfers between devices  149 us (6%)
  blocking collectives  55.8 us (2%)
  other arithmetic  28.3 us (1%)
    all_gather x1, waiting for transfers between devices, shards(): piece_blocks = lax.all_gather(row_tile, 'col', axis=1, tiled=True)  1100 us
    gather x32, local copies, waits for them, and re-layouts, one_block(): chosen = column_table[panel_steps[None, :], row_offsets]  575 us
    all_to_all x1, waiting for transfers between devices, shards(): lax.all_to_all(outgoing[0], ('col', 'layer'), split_axis=1, concat_axis=0...  297 us
    dot_general x16, matrix products, one_block(): jnp.einsum('mtab,mtsbc->msac', left_blocks, chosen, preferred_element_typ...  165 us
    all_to_all x1, starting transfers between devices, shards(): lax.all_to_all(outgoing[1], ('col', 'layer'), split_axis=1, concat_axis=0...  70 us
    all_to_all x1, starting transfers between devices, shards(): lax.all_to_all(col_tile, 'layer', split_axis=0, concat_axis=1, tiled=True)  59.9 us
    dynamic_update_slice x32, local copies, waits for them, and re-layouts, shards(): products = lax.map(one_block, jnp.arange(tile_rows // 8, dtype=jnp.int32))  54.4 us
  transfers between devices with their start and end apart: 8, of which 5 were waited for; matrix products, arithmetic and copies ran while one was open for 2% of the time, Pallas kernels for 0%

profile of v1, /device:TPU:0, one launch (start us, length us, event | category | flops | bytes accessed | tf_op | source)
XLA Modules:
  0.0 2610.0 jit_solution(8451826050809177474)
XLA Ops:
  35.6 296.6 %all-to-all-done.4 = bf16[16,16,2,128,128]{4,3,2,0,1:T(8,128)(2,1)} async-done(((bf16[16,16,2,128,128]{4,3,2,0,1:T(8,128)(2,1)}), bf16[16,16,2,128,128]{4,3,2,0,1:T(8,128)(2,1)}, u32[]{:S(2)}, u32[]{:S(2)}) %all-to-all-start.4) | async-done | bytes 16777248 | tf_op jit(solution)/shard_map/all_to_all | solution.py:62
  337.7 42.9 %scatter_fusion = bf16[128,2,128,128]{3,2,1,0:T(8,128)(2,1)} fusion(bf16[128,2,128,128]{3,2,1,0:T(8,128)(2,1)} %broadcast_in_dim.84, s32[256]{0:T(256)S(1)} %bitcast.95, bf16[256,2,128,128]{3,2,1,0:T(8,128)(2,1)} %bitcast.21), kind=kCustom, calls=%fused_computation.4 | custom fusion | bytes 50332672 | tf_op jit(solution)/shard_map/scatter | solution.py:78
  380.6 18.8 all_to_all.92
  412.0 70.0 %all-to-all-start.1 = ((s32[16,16,2]{0,2,1:T(2,128)}), s32[16,16,2]{0,2,1:T(2,128)S(1)}, u32[]{:S(2)}, u32[]{:S(2)}) async-start(s32[16,16,2]{0,2,1:T(2,128)} %bitcast.2), calls=%async_computation.1 | async-start | bytes 32768 | tf_op jit(solution)/shard_map/all_to_all | solution.py:63
  490.9 59.9 %all-to-all-start.2 = ((s32[2,1,128]{2,1,0:T(1,128)}), s32[2,1,128]{2,1,0:T(1,128)S(1)}, u32[]{:S(2)}, u32[]{:S(2)}) async-start(s32[2,1,128]{2,1,0:T(1,128)} %reshape.411), calls=%async_computation.2 | async-start | bytes 2048 | tf_op jit(solution)/shard_map/all_to_all | solution.py:87
  613.8 1100.1 %all-gather.4.cloned.1.call-done = bf16[128,16,128,128]{3,2,1,0:T(8,128)(2,1)} async-done(((bf16[128,2,128,128]{3,2,1,0:T(8,128)(2,1)}), bf16[128,16,128,128]{3,2,1,0:T(8,128)(2,1)}) %all-gather.4.cloned.1.call-update) | async-done | bytes 67108880 | tf_op jit(solution)/shard_map/all_gather | solution.py:98
  1713.9 835.0 %while.12 = (s32[]{:T(128)}, f32[16,8,4,128,128]{4,3,2,1,0:T(8,128)}, s32[16]{0:T(128)S(1)}, s32[128,16]{1,0:T(8,128)S(1)}, s32[16,8,4]{2,1,0:T(8,128)S(1)}, /*i...) while((s32[]{:T(128)}, ...), condition=%wide.region_4.5_spmd.clone, body=%wide.region_3.4_spmd.clone.sunk | while | flops 2155873536 | bytes 98579704 | solution.py:116
  1730.8 21.6 copy.59
  1783.0 21.6 copy.59
  1835.2 21.6 copy.59
  1887.4 21.6 copy.59
  1939.6 21.6 copy.59
  1991.8 21.6 copy.59
  2044.0 21.6 copy.59
  2096.3 21.6 copy.59
  2148.4 21.6 copy.59
  2200.6 21.6 copy.59
  2252.8 21.6 copy.59
  2304.9 21.6 copy.59
  2357.1 21.6 copy.59
  2409.3 21.6 copy.59
  2461.4 21.6 copy.59
  2513.6 21.6 copy.59
  2548.9 45.1 %reduce-scatter.2.cloned.1.call-done = f32[64,4,128,128]{3,2,1,0:T(8,128)} async-done(((f32[128,4,128,128]{3,2,1,0:T(8,128)}), f32[64,4,128,128]{3,2,1,0:T(8,128)}) %reduce-scatter.2.cloned.1.call-update) | async-done | bytes 16777232 | tf_op jit(solution)/shard_map/reduce_scatter | solution.py:118
  (239 shorter events, 606.7 us)
Async XLA Ops:
  7.8 21.5 all-to-all-start
  29.3 302.8 %all-to-all-start.4 = ((bf16[16,16,2,128,128]{4,3,2,0,1:T(8,128)(2,1)}), bf16[16,16,2,128,128]{4,3,2,0,1:T(8,128)(2,1)}, u32[]{:S(2)}, u32[]{:S(2)}) async-start(bf16[16,16,2,128,128]{4,3,2,0,1:T(8,128)(2,1)} %copy.40), calls=%async_computation.4 | async-start | bytes 33554432 | tf_op jit(solution)/shard_map/all_to_all | solution.py:62
  35.4 1678.6 %all-gather.4.cloned.1.call-start = ((), (), s32[]{:S(2)}) async-start(), calls=%async_computation.7 | async-start | bytes 75497472 | tf_op jit(solution)/shard_map/all_gather | solution.py:98
  380.6 30.8 %copy-start = (s32[16,32]{1,0:T(8,128)S(1)}, s32[16,32]{1,0:T(8,128)}, u32[]{:S(2)}) copy-start(s32[16,32]{1,0:T(8,128)} %param.7) | copy-start | bytes 6148
  409.8 186.8 %collective-permute-start = (bf16[1,64,4,128,128]{4,3,2,1,0:T(8,128)(2,1)}, bf16[1,64,4,128,128]{4,3,2,1,0:T(8,128)(2,1)}, u32[]{:S(2)}, u32[]{:S(2)}) collective-permute-start(bf16[1,64,4,128,128]{4,3,2,1,0:T(8,128)(2,1)} %bitcast.83), channel_id=1, source_target_pairs={{0,16},{16,0},{1,17},{17,1},{2,18},{18,2},{3,19},{19,3},{4,20},{20... | collective-permute-start | bytes 25165832 | tf_op jit(solution)/shard_map/ppermute | solution.py:20
  412.0 76.8 %all-to-all-start.1 = ((s32[16,16,2]{0,2,1:T(2,128)}), s32[16,16,2]{0,2,1:T(2,128)S(1)}, u32[]{:S(2)}, u32[]{:S(2)}) async-start(s32[16,16,2]{0,2,1:T(2,128)} %bitcast.2), calls=%async_computation.1 | async-start | bytes 32768 | tf_op jit(solution)/shard_map/all_to_all | solution.py:63
  490.9 78.4 %all-to-all-start.2 = ((s32[2,1,128]{2,1,0:T(1,128)}), s32[2,1,128]{2,1,0:T(1,128)S(1)}, u32[]{:S(2)}, u32[]{:S(2)}) async-start(s32[2,1,128]{2,1,0:T(1,128)} %reshape.411), calls=%async_computation.2 | async-start | bytes 2048 | tf_op jit(solution)/shard_map/all_to_all | solution.py:87
  569.3 25.0 all-to-all-start.3
  572.8 2021.2 %reduce-scatter.2.cloned.1.call-start = ((), (), s32[]{:S(2)}) async-start(), calls=%async_computation.8 | async-start | bytes 50331648 | tf_op jit(solution)/shard_map/reduce_scatter | solution.py:118
Sparse Core Ops, SparseCore 0:
  380.7 1333.1 all-gather.3
  2549.0 44.9 reduce-scatter.1
